TPU v7x, 256 devices: a whole 4x4x8 slice. The times are simulated.
256 devices in a mesh: slab: 64 (over y, x_lo, z), view: 4 (over x_hi, core).
Axes of the slice: x: 4 (x_hi: 2, x_lo: 2; x = x_hi * 2 + x_lo), y: 4, z: 8, core: 2. Of those that a mesh axis runs over, the one named last changes fastest.
Arguments:
- primal: float32 [5, 256, 32, 128], P(None, 'slab', 'view'), may hold values from -6 to 6
- dual: bfloat16 [64, 256, 128], P('view', 'slab'), may hold values from -6 to 6
- footprints: bfloat16 [8, 128, 128], replicated, may hold values from -0.046875 to 0.046875
- tile_index: int32 [64, 8192, 2], P(None, 'slab'), may hold values from 0 to 3
- footprint_offset: int32 [64, 8192, 2], P(None, 'slab'), may hold values from 0 to 7
- w_first: bfloat16 [3, 3, 3, 32, 6], replicated, may hold values from -0.21875 to 0.21875
- w_middle: bfloat16 [3, 3, 3, 32, 32], replicated, may hold values from -0.21875 to 0.21875
- w_last: bfloat16 [3, 3, 3, 5, 32], replicated, may hold values from -0.5 to 0.5
- cotangent: float32 [5, 256, 32, 128], P(None, 'slab', 'view'), may hold values from -6 to 6
Outputs:
- d_primal: float32 [5, 256, 32, 128], P(None, 'slab', 'view')
- d_dual: float32 [64, 256, 128], P('view', 'slab')
- d_first: float32 [3, 3, 3, 32, 6], replicated
- d_middle: float32 [3, 3, 3, 32, 32], replicated
- d_last: float32 [3, 3, 3, 5, 32], replicated
All inputs are finite; a program needn't handle non-finite values.
Results may differ from a plain program's by a relative error of at most 0.0067.
Values may be sent and summed in bfloat16 or wider, within the bound.
No kernel may reach another device: no remote copies, remote signals or barrier semaphores. Data moves between devices by JAX's collectives and lax.ppermute only.
A program may use at most 64 MiB of HBM per device.

v0:
```python
import math
import jax
import jax.numpy as jnp
from jax import lax
from jax.sharding import PartitionSpec as P


def with_halo(cells, sides, width):
    for axis, dim in sides:
        count = lax.axis_size(axis)
        ends = count - 1
        head = lax.slice_in_dim(cells, 0, width, axis=dim)
        tail = lax.slice_in_dim(cells, cells.shape[dim] - width, cells.shape[dim], axis=dim)
        cells = jnp.concatenate(
            [
                lax.ppermute(tail, axis, [(i, (i + 1) % count) for i in range(ends)]),
                cells,
                lax.ppermute(head, axis, [((i + 1) % count, i) for i in range(ends)]),
            ],
            axis=dim,
        )
    return cells


def silu_slope(value):
    sig = jax.nn.sigmoid(value)
    return sig * (1.0 + value * (1.0 - sig))


def flipped(kernel):
    return kernel[::-1, ::-1, ::-1].transpose(0, 1, 2, 4, 3)


def sideways(padded):
    blank = jnp.zeros(padded.shape[:-1] + (1,), padded.dtype)
    left = jnp.concatenate([blank, padded[..., :-1]], axis=-1)
    right = jnp.concatenate([padded[..., 1:], blank], axis=-1)
    return (left, padded, right)


def rims(field):
    return with_halo(field, (("slab", 1), ("view", 2)), 1)


def convolve(parts, kernel, depth, rows):
    total = None
    for za in range(3):
        for yb in range(3):
            for xc in range(3):
                term = jnp.einsum(
                    "oc,czyx->ozyx",
                    kernel[za, yb, xc],
                    parts[xc][:, za : za + depth, yb : yb + rows, :],
                    preferred_element_type=jnp.float32,
                )
                total = term if total is None else total + term
    return total


def kernel_grad(dout, parts, depth, rows):
    terms = []
    for za in range(3):
        for yb in range(3):
            for xc in range(3):
                terms.append(
                    jnp.einsum(
                        "ozyx,czyx->oc",
                        dout,
                        parts[xc][:, za : za + depth, yb : yb + rows, :],
                        preferred_element_type=jnp.float32,
                    )
                )
    return jnp.stack(terms).reshape(3, 3, 3, dout.shape[0], parts[0].shape[0])


def shards(
    primal, dual, footprints, tile_index, footprint_offset, w_first, w_middle, w_last, cotangent
):
    channels, depth, rows_here, width = primal.shape
    views_here, det_tiles, bins = dual.shape
    all_views = tile_index.shape[0]
    taps = tile_index.shape[2]
    foot_count = footprints.shape[0]
    n_view = lax.axis_size("view")
    full_rows = rows_here * n_view
    x_tiles = width // bins
    view_at = lax.axis_index("view")
    forward_mat = footprints.transpose(1, 0, 2).reshape(bins, foot_count * bins)
    backward_mat = footprints.transpose(2, 0, 1).reshape(bins, foot_count * bins)
    tile_grid = tile_index.reshape(all_views, depth, full_rows, x_tiles, taps)
    foot_grid = footprint_offset.reshape(all_views, depth, full_rows, x_tiles, taps)
    stride = det_tiles * foot_count
    heights = jnp.dot(
        dual.reshape(-1, bins), forward_mat, preferred_element_type=jnp.float32
    ).reshape(-1, bins)
    own_tiles = lax.dynamic_slice_in_dim(tile_grid, view_at * views_here, views_here, 0)
    own_foot = lax.dynamic_slice_in_dim(foot_grid, view_at * views_here, views_here, 0)
    count = rows_here * lax.axis_size("view")

    def strip_add_view(view, total):
        picks = view * stride + own_tiles[view] * foot_count + own_foot[view]
        return total + jnp.take(heights, picks, axis=0).sum(axis=3)

    total = lax.fori_loop(
        0, views_here, strip_add_view, jnp.zeros((depth, count, x_tiles, bins), jnp.float32)
    )
    strips = lax.psum_scatter(
        total.reshape(depth, count, width).transpose(1, 0, 2),
        "view",
        scatter_dimension=0,
        tiled=True,
    )
    back = strips.transpose(1, 0, 2)
    x_zero = jnp.concatenate([primal, back[None]], axis=0).astype(jnp.bfloat16)
    g_low = cotangent.astype(jnp.bfloat16)
    x_parts = sideways(with_halo(x_zero, (("slab", 1), ("view", 2)), 1))
    g_parts = sideways(with_halo(g_low, (("slab", 1), ("view", 2)), 1))
    a_one = convolve(x_parts, w_first, depth, rows_here)
    z_one = jax.nn.silu(a_one).astype(jnp.bfloat16)
    z_one_parts = sideways(rims(z_one))
    a_two = convolve(z_one_parts, w_middle, depth, rows_here)
    z_two = jax.nn.silu(a_two).astype(jnp.bfloat16)
    z_two_parts = sideways(rims(z_two))
    dz_two = convolve(g_parts, flipped(w_last), depth, rows_here)
    d_last = kernel_grad(g_low, z_two_parts, depth, rows_here)
    da_two = (dz_two * silu_slope(a_two)).astype(jnp.bfloat16)
    dz_one = convolve(sideways(rims(da_two)), flipped(w_middle), depth, rows_here)
    d_middle = kernel_grad(da_two, z_one_parts, depth, rows_here)
    da_one = (dz_one * silu_slope(a_one)).astype(jnp.bfloat16)
    dx_zero = convolve(sideways(rims(da_one)), flipped(w_first), depth, rows_here)
    d_first = kernel_grad(da_one, x_parts, depth, rows_here)
    d_primal = cotangent + dx_zero[:channels]
    strip_grad = dx_zero[channels].astype(jnp.bfloat16)
    start_grad = jnp.zeros((views_here * det_tiles, bins), jnp.float32)
    piece = lax.all_gather(strip_grad, "view", axis=1, tiled=True)
    count = piece.shape[1]
    proj = jnp.dot(
        piece.reshape(-1, bins), backward_mat, preferred_element_type=jnp.float32
    ).reshape(-1, bins)
    tile_ids = jnp.arange(depth * count * x_tiles, dtype=jnp.int32).reshape(
        depth, count, x_tiles, 1
    )

    def fold_add_view(view, acc):
        source = tile_ids * foot_count + own_foot[view]
        target = view * det_tiles + own_tiles[view]
        return acc + jax.ops.segment_sum(
            jnp.take(proj, source.reshape(-1), axis=0),
            target.reshape(-1),
            num_segments=views_here * det_tiles,
        )

    d_dual = lax.fori_loop(0, views_here, fold_add_view, start_grad).reshape(
        views_here, det_tiles, bins
    )
    summed = lax.psum((d_first, d_middle, d_last), ("slab", "view"))
    scale = 1.0 / math.sqrt(depth * lax.axis_size("slab") * full_rows * width)
    return (d_primal, d_dual, summed[0] * scale, summed[1] * scale, summed[2] * scale)


def solution(mesh):
    placed = (
        P(None, "slab", "view", None),
        P("view", "slab", None),
        P(),
        P(None, "slab", None),
        P(None, "slab", None),
        P(),
        P(),
        P(),
        P(None, "slab", "view", None),
    )
    return jax.shard_map(
        shards,
        mesh=mesh,
        in_specs=placed,
        out_specs=(P(None, "slab", "view", None), P("view", "slab", None), P(), P(), P()),
        check_vma=False,
    )
```

profile of v0, /device:TPU:1, one launch (start us, length us, event | category | flops | bytes accessed | tf_op | source)
XLA Modules:
  0.0 618.3 jit_solution(12563308730298618970)
XLA Ops:
  7.3 3.5 copy.388
  10.8 2.7 copy.389
  15.7 21.8 %while.30 = (s32[]{:T(128)}, f32[4,32,1,128]{3,2,1,0:T(1,128)S(1)}, s32[16,4,32,1,2]{4,2,1,3,0:T(8,128)S(1)}, s32[16,4,32,1,2]{4,2,1,3,0:T(8,128)S(1)}, f32[512,...) while((s32[]{:T(128)}, f32[4,32,1,128]{3,2,1,0:T(1,128)S(1)}, ...), condition=%wide.region_2.3_spmd.clone, body=%wide.region_0.2_spmd.clone.sunk | while | flops 86788 | bytes 669307 | solution.py:104
  38.3 4.4 collective-permute-start
  44.8 2.4 collective-permute-done.1
  47.3 6.5 %collective-permute-start.2 = (bf16[5,6,1,128]{3,2,1,0:T(2,128)(2,1)S(1)}, bf16[5,6,1,128]{3,2,1,0:T(2,128)(2,1)S(1)}, u32[]{:S(2)}, u32[]{:S(2)}) collective-permute-start(bf16[5,6,1,128]{3,2,1,0:T(2,128)(2,1)S(1)} %get-tuple-element.443), channel_id=1, source_target_pairs={{0,1},{1,2},{2,3},{4,5},{5,6},{6,7},{8,9},{9,10},{10,11},{12,13},{... | collective-permute-start | bytes 23048 | tf_op jit(solution)/shard_map/ppermute | solution.py:16
  53.7 1.9 collective-permute-start.3
  55.7 4.6 collective-permute-done.3
  68.7 4.5 reduce-scatter.2.cloned.1.call-done
  73.9 3.2 collective-permute-start.4
  79.4 2.1 collective-permute-done.5
  81.5 4.7 collective-permute-start.6
  86.3 1.9 collective-permute-start.7
  88.3 4.6 collective-permute-done.7
  106.4 3.2 collective-permute-start.8
  112.3 2.8 collective-permute-done.9
  115.2 3.1 collective-permute-start.10
  120.3 4.9 collective-permute-done.11
  158.0 4.8 collective-permute-start.20
  164.1 4.3 collective-permute-start.12
  169.7 240.3 %all-reduce.15.cloned.1.call-done = f32[3,3,3,32,32]{4,3,2,1,0:T(8,128)} async-done(((f32[3,3,3,32,32]{4,3,2,1,0:T(8,128)}), f32[3,3,3,32,32]{4,3,2,1,0:T(8,128)}) %all-reduce.15.cloned.1.call-update) | async-done | bytes 110608 | tf_op jit(solution)/shard_map/psum | solution.py:156
  411.8 5.5 collective-permute-start.22
  417.3 1.9 collective-permute-start.23
  419.3 5.1 collective-permute-start.14
  424.5 2.1 collective-permute-start.15
  426.6 4.8 collective-permute-done.15
  453.8 80.9 %all-reduce.12 = (f32[3,3,3,32,6]{3,4,2,1,0:T(8,128)S(1)}, f32[3,3,3,5,32]{4,2,3,1,0:T(4,128)S(1)}) all-reduce(f32[3,3,3,32,6]{3,4,2,1,0:T(8,128)} %bitcast.1969, f32[3,3,3,5,32]{4,2,3,1,0:T(4,128)S(1)} %copy.582), channel_id=1, replica_groups=mesh['slab'=64,'view'=4] {'slab','view'}, use_global_device_ids=true, to_apply=%region_7.8 | all-reduce | flops 9504 | bytes 76032 | tf_op jit(solution)/shard_map/psum | solution.py:156
  535.4 3.8 collective-permute-start.18
  539.2 2.1 collective-permute-start.19
  542.0 4.1 collective-permute-done.19
  551.5 5.6 all-gather
  557.4 53.1 %while.29 = (s32[]{:T(128)}, f32[64,128]{1,0:T(8,128)S(1)}, s32[16,4,32,1,2]{4,2,1,3,0:T(8,128)S(1)}, s32[16,4,32,1,2]{4,2,1,3,0:T(8,128)S(1)}, f32[1024,128]{1,...) while((s32[]{:T(128)}, f32[64,128]{1,0:T(8,128)S(1)}, ...), condition=%wide.region_6.7_spmd.clone.clone, body=%wide.region_4.6_spmd.clone.clone.sunk | while | flops 70019 | bytes 588653 | solution.py:153
  558.3 2.4 scatter_custom_fusion.6
  561.6 2.4 scatter_custom_fusion.6
  565.0 2.4 scatter_custom_fusion.6
  568.3 2.4 scatter_custom_fusion.6
  571.6 2.4 scatter_custom_fusion.6
  574.9 2.4 scatter_custom_fusion.6
  578.2 2.4 scatter_custom_fusion.6
  581.5 2.4 scatter_custom_fusion.6
  584.9 2.4 scatter_custom_fusion.6
  588.2 2.4 scatter_custom_fusion.6
  591.5 2.4 scatter_custom_fusion.6
  594.8 2.4 scatter_custom_fusion.6
  598.1 2.4 scatter_custom_fusion.6
  601.4 2.4 scatter_custom_fusion.6
  604.8 2.4 scatter_custom_fusion.6
  608.1 2.4 scatter_custom_fusion.6
  (727 shorter events, 134.8 us)
Async XLA Ops:
  7.2 66.0 %reduce-scatter.2.cloned.1.call-start = ((), (), s32[]{:S(2)}) async-start(), calls=%async_computation.1 | async-start | bytes 81920 | tf_op jit(solution)/shard_map/reduce_scatter | solution.py:107
  15.7 22.5 %copy-start.6 = (f32[5,4,8,128]{3,2,1,0:T(8,128)S(1)}, f32[5,4,8,128]{3,2,1,0:T(8,128)}, u32[]{:S(2)}) copy-start(f32[5,4,8,128]{3,2,1,0:T(8,128)} %param.21) | copy-start | bytes 245764
  15.7 28.2 %copy-start.58 = (bf16[3,3,3,5,32]{4,2,3,1,0:T(4,128)(2,1)S(1)}, bf16[3,3,3,5,32]{4,2,3,1,0:T(4,128)(2,1)}, u32[]{:S(2)}) copy-start(bf16[3,3,3,5,32]{4,2,3,1,0:T(4,128)(2,1)} %param.20) | copy-start | bytes 25924
  15.7 28.3 %copy-start.5 = (bf16[3,3,3,32,32]{4,3,2,1,0:T(8,128)(2,1)S(1)}, bf16[3,3,3,32,32]{4,3,2,1,0:T(8,128)(2,1)}, u32[]{:S(2)}) copy-start(bf16[3,3,3,32,32]{4,3,2,1,0:T(8,128)(2,1)} %param.19) | copy-start | bytes 165892
  15.7 28.5 %copy-start.49 = (bf16[3,3,3,32,6]{3,4,2,1,0:T(8,128)(2,1)S(1)}, bf16[3,3,3,32,6]{3,4,2,1,0:T(8,128)(2,1)}, u32[]{:S(2)}) copy-start(bf16[3,3,3,32,6]{3,4,2,1,0:T(8,128)(2,1)} %param.18) | copy-start | bytes 31108
  15.7 29.1 %copy-start.54 = (f32[5,4,8,128]{3,2,1,0:T(8,128)S(1)}, f32[5,4,8,128]{3,2,1,0:T(8,128)}, u32[]{:S(2)}) copy-start(f32[5,4,8,128]{3,2,1,0:T(8,128)} %param.13) | copy-start | bytes 245764
  38.2 371.8 %all-reduce.15.cloned.1.call-start = ((), (), s32[]{:S(2)}) async-start(), calls=%async_computation.2 | async-start | bytes 884736 | tf_op jit(solution)/shard_map/psum | solution.py:156
  38.3 6.6 %collective-permute-start = (bf16[5,1,8,128]{3,2,1,0:T(8,128)(2,1)S(1)}, bf16[5,1,8,128]{3,2,1,0:T(8,128)(2,1)S(1)}, u32[]{:S(2)}, u32[]{:S(2)}) collective-permute-start(bf16[5,1,8,128]{3,2,1,0:T(8,128)(2,1)S(1)} %get-tuple-element.452), channel_id=1, source_target_pairs={{0,4},{4,8},{8,12},{12,16},{16,20},{20,24},{24,28},{28,32},{32,36}... | collective-permute-start | bytes 30728 | tf_op jit(solution)/shard_map/ppermute | solution.py:16
  42.6 4.6 collective-permute-start.1
  44.0 23.4 %copy-start.51 = (bf16[3,3,3,32,5]{3,4,2,1,0:T(8,128)(2,1)}, bf16[3,3,3,32,5]{3,4,2,1,0:T(8,128)(2,1)S(1)}, u32[]{:S(2)}) copy-start(bf16[3,3,3,32,5]{3,4,2,1,0:T(8,128)(2,1)S(1)} %reverse_bitcast_fusion.2) | copy-start | bytes 25924
  47.3 8.4 %collective-permute-start.2 = (bf16[5,6,1,128]{3,2,1,0:T(2,128)(2,1)S(1)}, bf16[5,6,1,128]{3,2,1,0:T(2,128)(2,1)S(1)}, u32[]{:S(2)}, u32[]{:S(2)}) collective-permute-start(bf16[5,6,1,128]{3,2,1,0:T(2,128)(2,1)S(1)} %get-tuple-element.443), channel_id=1, source_target_pairs={{0,1},{1,2},{2,3},{4,5},{5,6},{6,7},{8,9},{9,10},{10,11},{12,13},{... | collective-permute-start | bytes 23048 | tf_op jit(solution)/shard_map/ppermute | solution.py:16
  53.7 6.6 %collective-permute-start.3 = (bf16[5,6,1,128]{3,2,1,0:T(2,128)(2,1)S(1)}, bf16[5,6,1,128]{3,2,1,0:T(2,128)(2,1)S(1)}, u32[]{:S(2)}, u32[]{:S(2)}) collective-permute-start(bf16[5,6,1,128]{3,2,1,0:T(2,128)(2,1)S(1)} %get-tuple-element.444), channel_id=1, source_target_pairs={{1,0},{2,1},{3,2},{5,4},{6,5},{7,6},{9,8},{10,9},{11,10},{13,12},{... | collective-permute-start | bytes 23048 | tf_op jit(solution)/shard_map/ppermute | solution.py:18
  73.9 5.5 collective-permute-start.4
  77.1 4.4 collective-permute-start.5
  78.4 21.2 %copy-start.50 = (bf16[3,3,3,32,6]{3,4,2,1,0:T(8,128)(2,1)S(1)}, bf16[3,3,3,32,6]{3,4,2,1,0:T(8,128)(2,1)}, u32[]{:S(2)}) copy-start(bf16[3,3,3,32,6]{3,4,2,1,0:T(8,128)(2,1)} %param.18) | copy-start | bytes 31108
  81.5 6.7 %collective-permute-start.6 = (bf16[6,6,1,128]{3,2,1,0:T(2,128)(2,1)S(1)}, bf16[6,6,1,128]{3,2,1,0:T(2,128)(2,1)S(1)}, u32[]{:S(2)}, u32[]{:S(2)}) collective-permute-start(bf16[6,6,1,128]{3,2,1,0:T(2,128)(2,1)S(1)} %get-tuple-element.440), channel_id=1, source_target_pairs={{0,1},{1,2},{2,3},{4,5},{5,6},{6,7},{8,9},{9,10},{10,11},{12,13},{... | collective-permute-start | bytes 27656 | tf_op jit(solution)/shard_map/ppermute | solution.py:16
  86.3 6.6 %collective-permute-start.7 = (bf16[6,6,1,128]{3,2,1,0:T(2,128)(2,1)S(1)}, bf16[6,6,1,128]{3,2,1,0:T(2,128)(2,1)S(1)}, u32[]{:S(2)}, u32[]{:S(2)}) collective-permute-start(bf16[6,6,1,128]{3,2,1,0:T(2,128)(2,1)S(1)} %get-tuple-element.439), channel_id=1, source_target_pairs={{1,0},{2,1},{3,2},{5,4},{6,5},{7,6},{9,8},{10,9},{11,10},{13,12},{... | collective-permute-start | bytes 27656 | tf_op jit(solution)/shard_map/ppermute | solution.py:18
  88.2 12.0 %copy-start.17 = (bf16[6,4,8,128]{3,2,1,0:T(8,128)(2,1)}, bf16[6,4,8,128]{3,2,1,0:T(8,128)(2,1)S(1)}, u32[]{:S(2)}) copy-start(bf16[6,4,8,128]{3,2,1,0:T(8,128)(2,1)S(1)} %get-tuple-element.446) | copy-start | bytes 147460
  93.3 7.2 %copy-start.25 = (bf16[6,4,8,128]{3,2,1,0:T(8,128)(2,1)}, bf16[6,4,8,128]{3,2,1,0:T(8,128)(2,1)S(1)}, u32[]{:S(2)}) copy-start(bf16[6,4,8,128]{3,2,1,0:T(8,128)(2,1)S(1)} %get-tuple-element.399) | copy-start | bytes 147460
  93.3 8.0 %copy-start.21 = (bf16[6,4,8,128]{3,2,1,0:T(8,128)(2,1)}, bf16[6,4,8,128]{3,2,1,0:T(8,128)(2,1)S(1)}, u32[]{:S(2)}) copy-start(bf16[6,4,8,128]{3,2,1,0:T(8,128)(2,1)S(1)} %get-tuple-element.400) | copy-start | bytes 147460
  93.3 8.9 %copy-start.15 = (bf16[6,4,8,128]{3,2,1,0:T(8,128)(2,1)}, bf16[6,4,8,128]{3,2,1,0:T(8,128)(2,1)S(1)}, u32[]{:S(2)}) copy-start(bf16[6,4,8,128]{3,2,1,0:T(8,128)(2,1)S(1)} %get-tuple-element.401) | copy-start | bytes 147460
  93.3 9.7 %copy-start.7 = (bf16[6,4,8,128]{3,2,1,0:T(8,128)(2,1)}, bf16[6,4,8,128]{3,2,1,0:T(8,128)(2,1)S(1)}, u32[]{:S(2)}) copy-start(bf16[6,4,8,128]{3,2,1,0:T(8,128)(2,1)S(1)} %get-tuple-element.402) | copy-start | bytes 147460
  94.5 7.2 %copy-start.31 = (bf16[6,4,8,128]{3,2,1,0:T(8,128)(2,1)}, bf16[6,4,8,128]{3,2,1,0:T(8,128)(2,1)S(1)}, u32[]{:S(2)}) copy-start(bf16[6,4,8,128]{3,2,1,0:T(8,128)(2,1)S(1)} %get-tuple-element.406) | copy-start | bytes 147460
  94.6 7.3 %copy-start.35 = (bf16[6,4,8,128]{3,2,1,0:T(8,128)(2,1)}, bf16[6,4,8,128]{3,2,1,0:T(8,128)(2,1)S(1)}, u32[]{:S(2)}) copy-start(bf16[6,4,8,128]{3,2,1,0:T(8,128)(2,1)S(1)} %get-tuple-element.388) | copy-start | bytes 147460
  94.7 8.1 %copy-start.27 = (bf16[6,4,8,128]{3,2,1,0:T(8,128)(2,1)}, bf16[6,4,8,128]{3,2,1,0:T(8,128)(2,1)S(1)}, u32[]{:S(2)}) copy-start(bf16[6,4,8,128]{3,2,1,0:T(8,128)(2,1)S(1)} %get-tuple-element.389) | copy-start | bytes 147460
  94.7 9.0 %copy-start.19 = (bf16[6,4,8,128]{3,2,1,0:T(8,128)(2,1)}, bf16[6,4,8,128]{3,2,1,0:T(8,128)(2,1)S(1)}, u32[]{:S(2)}) copy-start(bf16[6,4,8,128]{3,2,1,0:T(8,128)(2,1)S(1)} %get-tuple-element.391) | copy-start | bytes 147460
  94.7 9.8 %copy-start.9 = (bf16[6,4,8,128]{3,2,1,0:T(8,128)(2,1)}, bf16[6,4,8,128]{3,2,1,0:T(8,128)(2,1)S(1)}, u32[]{:S(2)}) copy-start(bf16[6,4,8,128]{3,2,1,0:T(8,128)(2,1)S(1)} %get-tuple-element.392) | copy-start | bytes 147460
  94.7 10.6 %copy-start.56 = (bf16[6,4,8,128]{3,2,1,0:T(8,128)(2,1)}, bf16[6,4,8,128]{3,2,1,0:T(8,128)(2,1)S(1)}, u32[]{:S(2)}) copy-start(bf16[6,4,8,128]{3,2,1,0:T(8,128)(2,1)S(1)} %get-tuple-element.385) | copy-start | bytes 147460
  95.7 7.6 %copy-start.33 = (bf16[6,4,8,128]{3,2,1,0:T(8,128)(2,1)}, bf16[6,4,8,128]{3,2,1,0:T(8,128)(2,1)S(1)}, u32[]{:S(2)}) copy-start(bf16[6,4,8,128]{3,2,1,0:T(8,128)(2,1)S(1)} %get-tuple-element.395) | copy-start | bytes 147460
  95.8 9.3 %copy-start.13 = (bf16[6,4,8,128]{3,2,1,0:T(8,128)(2,1)}, bf16[6,4,8,128]{3,2,1,0:T(8,128)(2,1)S(1)}, u32[]{:S(2)}) copy-start(bf16[6,4,8,128]{3,2,1,0:T(8,128)(2,1)S(1)} %get-tuple-element.394) | copy-start | bytes 147460
  106.4 5.9 collective-permute-start.8
  109.6 5.6 collective-permute-start.9
  115.2 5.1 collective-permute-start.10
  118.3 6.9 %collective-permute-start.11 = (bf16[32,6,1,128]{3,0,2,1:T(8,128)(2,1)S(1)}, bf16[32,6,1,128]{3,0,2,1:T(8,128)(2,1)S(1)}, u32[]{:S(2)}, u32[]{:S(2)}) collective-permute-start(bf16[32,6,1,128]{3,0,2,1:T(8,128)(2,1)S(1)} %get-tuple-element.372), channel_id=1, source_target_pairs={{1,0},{2,1},{3,2},{5,4},{6,5},{7,6},{9,8},{10,9},{11,10},{13,12},{... | collective-permute-start | bytes 147464 | tf_op jit(solution)/shard_map/ppermute | solution.py:18
  158.0 253.8 %collective-permute-start.20 = (bf16[32,1,8,128]{3,0,2,1:T(8,128)(2,1)}, bf16[32,1,8,128]{3,0,2,1:T(8,128)(2,1)S(1)}, u32[]{:S(2)}, u32[]{:S(2)}) collective-permute-start(bf16[32,1,8,128]{3,0,2,1:T(8,128)(2,1)} %get-tuple-element.375), channel_id=1, source_target_pairs={{0,4},{4,8},{8,12},{12,16},{16,20},{20,24},{24,28},{28,32},{32,36}... | collective-permute-start | bytes 196616 | tf_op jit(solution)/shard_map/ppermute | solution.py:16
  162.8 249.0 %collective-permute-start.21 = (bf16[32,1,8,128]{3,0,2,1:T(8,128)(2,1)}, bf16[32,1,8,128]{3,0,2,1:T(8,128)(2,1)S(1)}, u32[]{:S(2)}, u32[]{:S(2)}) collective-permute-start(bf16[32,1,8,128]{3,0,2,1:T(8,128)(2,1)} %get-tuple-element.376), channel_id=1, source_target_pairs={{4,0},{8,4},{12,8},{16,12},{20,16},{24,20},{28,24},{32,28},{36,32}... | collective-permute-start | bytes 196616 | tf_op jit(solution)/shard_map/ppermute | solution.py:18
  164.1 255.2 %collective-permute-start.12 = (bf16[32,1,8,128]{3,0,2,1:T(8,128)(2,1)}, bf16[32,1,8,128]{3,0,2,1:T(8,128)(2,1)S(1)}, u32[]{:S(2)}, u32[]{:S(2)}) collective-permute-start(bf16[32,1,8,128]{3,0,2,1:T(8,128)(2,1)} %get-tuple-element.379), channel_id=1, source_target_pairs={{0,4},{4,8},{8,12},{12,16},{16,20},{20,24},{24,28},{28,32},{32,36}... | collective-permute-start | bytes 196616 | tf_op jit(solution)/shard_map/ppermute | solution.py:16
  168.4 250.9 %collective-permute-start.13 = (bf16[32,1,8,128]{3,0,2,1:T(8,128)(2,1)}, bf16[32,1,8,128]{3,0,2,1:T(8,128)(2,1)S(1)}, u32[]{:S(2)}, u32[]{:S(2)}) collective-permute-start(bf16[32,1,8,128]{3,0,2,1:T(8,128)(2,1)} %get-tuple-element.380), channel_id=1, source_target_pairs={{4,0},{8,4},{12,8},{16,12},{20,16},{24,20},{28,24},{32,28},{36,32}... | collective-permute-start | bytes 196616 | tf_op jit(solution)/shard_map/ppermute | solution.py:18
  411.8 27.3 %collective-permute-start.22 = (bf16[32,6,1,128]{3,0,2,1:T(8,128)(2,1)S(1)}, bf16[32,6,1,128]{3,0,2,1:T(8,128)(2,1)S(1)}, u32[]{:S(2)}, u32[]{:S(2)}) collective-permute-start(bf16[32,6,1,128]{3,0,2,1:T(8,128)(2,1)S(1)} %get-tuple-element.361), channel_id=1, source_target_pairs={{0,1},{1,2},{2,3},{4,5},{5,6},{6,7},{8,9},{9,10},{10,11},{12,13},{... | collective-permute-start | bytes 147464 | tf_op jit(solution)/shard_map/ppermute | solution.py:16
  417.3 21.8 %collective-permute-start.23 = (bf16[32,6,1,128]{3,0,2,1:T(8,128)(2,1)S(1)}, bf16[32,6,1,128]{3,0,2,1:T(8,128)(2,1)S(1)}, u32[]{:S(2)}, u32[]{:S(2)}) collective-permute-start(bf16[32,6,1,128]{3,0,2,1:T(8,128)(2,1)S(1)} %get-tuple-element.362), channel_id=1, source_target_pairs={{1,0},{2,1},{3,2},{5,4},{6,5},{7,6},{9,8},{10,9},{11,10},{13,12},{... | collective-permute-start | bytes 147464 | tf_op jit(solution)/shard_map/ppermute | solution.py:18
  419.3 7.3 %collective-permute-start.14 = (bf16[32,6,1,128]{3,0,2,1:T(8,128)(2,1)S(1)}, bf16[32,6,1,128]{3,0,2,1:T(8,128)(2,1)S(1)}, u32[]{:S(2)}, u32[]{:S(2)}) collective-permute-start(bf16[32,6,1,128]{3,0,2,1:T(8,128)(2,1)S(1)} %get-tuple-element.367), channel_id=1, source_target_pairs={{0,1},{1,2},{2,3},{4,5},{5,6},{6,7},{8,9},{9,10},{10,11},{12,13},{... | collective-permute-start | bytes 147464 | tf_op jit(solution)/shard_map/ppermute | solution.py:16
  424.5 6.9 %collective-permute-start.15 = (bf16[32,6,1,128]{3,0,2,1:T(8,128)(2,1)S(1)}, bf16[32,6,1,128]{3,0,2,1:T(8,128)(2,1)S(1)}, u32[]{:S(2)}, u32[]{:S(2)}) collective-permute-start(bf16[32,6,1,128]{3,0,2,1:T(8,128)(2,1)S(1)} %get-tuple-element.368), channel_id=1, source_target_pairs={{1,0},{2,1},{3,2},{5,4},{6,5},{7,6},{9,8},{10,9},{11,10},{13,12},{... | collective-permute-start | bytes 147464 | tf_op jit(solution)/shard_map/ppermute | solution.py:18
  450.9 84.4 %collective-permute-start.16 = (bf16[32,1,8,128]{3,0,2,1:T(8,128)(2,1)}, bf16[32,1,8,128]{3,0,2,1:T(8,128)(2,1)S(1)}, u32[]{:S(2)}, u32[]{:S(2)}) collective-permute-start(bf16[32,1,8,128]{3,0,2,1:T(8,128)(2,1)} %get-tuple-element.377), channel_id=1, source_target_pairs={{0,4},{4,8},{8,12},{12,16},{16,20},{20,24},{24,28},{28,32},{32,36}... | collective-permute-start | bytes 196616 | tf_op jit(solution)/shard_map/ppermute | solution.py:16
  452.3 83.0 %collective-permute-start.17 = (bf16[32,1,8,128]{3,0,2,1:T(8,128)(2,1)}, bf16[32,1,8,128]{3,0,2,1:T(8,128)(2,1)S(1)}, u32[]{:S(2)}, u32[]{:S(2)}) collective-permute-start(bf16[32,1,8,128]{3,0,2,1:T(8,128)(2,1)} %get-tuple-element.378), channel_id=1, source_target_pairs={{4,0},{8,4},{12,8},{16,12},{20,16},{24,20},{28,24},{32,28},{36,32}... | collective-permute-start | bytes 196616 | tf_op jit(solution)/shard_map/ppermute | solution.py:18
  535.4 6.6 %collective-permute-start.18 = (bf16[32,6,1,128]{3,0,2,1:T(8,128)(2,1)S(1)}, bf16[32,6,1,128]{3,0,2,1:T(8,128)(2,1)S(1)}, u32[]{:S(2)}, u32[]{:S(2)}) collective-permute-start(bf16[32,6,1,128]{3,0,2,1:T(8,128)(2,1)S(1)} %get-tuple-element.363), channel_id=1, source_target_pairs={{0,1},{1,2},{2,3},{4,5},{5,6},{6,7},{8,9},{9,10},{10,11},{12,13},{... | collective-permute-start | bytes 147464 | tf_op jit(solution)/shard_map/ppermute | solution.py:16
  539.2 6.9 %collective-permute-start.19 = (bf16[32,6,1,128]{3,0,2,1:T(8,128)(2,1)S(1)}, bf16[32,6,1,128]{3,0,2,1:T(8,128)(2,1)S(1)}, u32[]{:S(2)}, u32[]{:S(2)}) collective-permute-start(bf16[32,6,1,128]{3,0,2,1:T(8,128)(2,1)S(1)} %get-tuple-element.364), channel_id=1, source_target_pairs={{1,0},{2,1},{3,2},{5,4},{6,5},{7,6},{9,8},{10,9},{11,10},{13,12},{... | collective-permute-start | bytes 147464 | tf_op jit(solution)/shard_map/ppermute | solution.py:18
  549.8 7.3 %copy-start.4 = (bf16[8,128,128]{2,1,0:T(8,128)(2,1)S(1)}, bf16[8,128,128]{2,1,0:T(8,128)(2,1)}, u32[]{:S(2)}) copy-start(bf16[8,128,128]{2,1,0:T(8,128)(2,1)} %param.15) | copy-start | bytes 786436
  557.1 54.1 %copy-start.1 = (bf16[16,4,128]{2,1,0:T(4,128)(2,1)S(1)}, bf16[16,4,128]{2,1,0:T(4,128)(2,1)}, u32[]{:S(2)}) copy-start(bf16[16,4,128]{2,1,0:T(4,128)(2,1)} %param.14) | copy-start | bytes 49156
  (40 other events, 154.0 us)
Sparse Core Ops, SparseCore 0:
  38.3 34.8 reduce-scatter.1
  157.4 252.5 all-reduce.14
where the time goes:
time: 628 us; the launch traced here: 618 us
  waiting for transfers between devices  275 us (44%)
  blocking collectives  86.5 us (14%)
  matrix products  72.4 us (12%)
  starting transfers between devices  70.2 us (11%)
  other arithmetic  51.7 us (8%)
  local copies, waits for them, and re-layouts  44 us (7%)
  between operations  16.3 us (3%)
    psum x1, waiting for transfers between devices, shards(): summed = lax.psum((d_first, d_middle, d_last), ('slab', 'view'))  240 us
    psum x1, blocking collectives, shards(): summed = lax.psum((d_first, d_middle, d_last), ('slab', 'view'))  80.9 us
    ppermute x12, starting transfers between devices, with_halo(): lax.ppermute(tail, axis, [(i, (i + 1) % count) for i in range(ends)])  50 us
    dot_general x135, matrix products, convolve(): jnp.einsum('oc,czyx->ozyx', kernel[za, yb, xc], parts[xc][:, za:za + dept...  40 us
    scatter-add x16, other arithmetic, fold_add_view(): jax.ops.segment_sum(jnp.take(proj, source.reshape(-1), axis=0), target.re...  38.8 us
    dot_general x81, matrix products, kernel_grad(): jnp.einsum('ozyx,czyx->oc', dout, parts[xc][:, za:za + depth, yb:yb + row...  31.9 us
    ppermute x12, waiting for transfers between devices, with_halo(): lax.ppermute(head, axis, [((i + 1) % count, i) for i in range(ends)])  30.4 us
    ppermute x12, starting transfers between devices, with_halo(): lax.ppermute(head, axis, [((i + 1) % count, i) for i in range(ends)])  20.1 us
  transfers between devices with their start and end apart: 26, of which 10 were waited for; matrix products, arithmetic and copies ran while one was open for 4% of the time, Pallas kernels for 0%

commit v1 on v0

--- a/solution.py
+++ b/solution.py
@@ -153,7 +153,7 @@
     d_dual = lax.fori_loop(0, views_here, fold_add_view, start_grad).reshape(
         views_here, det_tiles, bins
     )
-    summed = lax.psum((d_first, d_middle, d_last), ("slab", "view"))
+    summed = lax.psum(lax.psum((d_first, d_middle, d_last), "view"), "slab")
     scale = 1.0 / math.sqrt(depth * lax.axis_size("slab") * full_rows * width)
     return (d_primal, d_dual, summed[0] * scale, summed[1] * scale, summed[2] * scale)
 

time: 628 us -> 890 us (1.42)
  blocking collectives: 86.5 us -> 321 us
  starting transfers between devices: 70.2 us -> 122 us
  waiting for transfers between devices: 275 us -> 231 us
  matrix products: 72.4 us -> 87.1 us
    psum x1 -> x2, blocking collectives: 80.9 us -> 273 us  [shards(): summed = lax.psum(lax.psum((d_first, d_middle, d_last), 'view'), 'slab')]
    ppermute x12, starting transfers between devices: 50 us -> 101 us  [with_halo(): lax.ppermute(tail, axis, [(i, (i + 1) % count) for i in range(ends)])]
    all_gather x1, blocking collectives: 5.59 us -> 48.3 us  [shards(): piece = lax.all_gather(strip_grad, 'view', axis=1, tiled=True)]
    psum x1 -> x2, waiting for transfers between devices: 240 us -> 200 us  [shards(): summed = lax.psum(lax.psum((d_first, d_middle, d_last), 'view'), 'slab')]
    dot_general x81, matrix products: 31.9 us -> 48 us  [kernel_grad(): jnp.einsum('ozyx,czyx->oc', dout, parts[xc][:, za:za + depth, yb:yb + row...]
  transfers between devices with their start and end apart: 26 -> 27, of which waited for: 10 -> 10; matrix products, arithmetic and copies ran while one was open for 4% -> 7% of each run, Pallas kernels for 0% -> 0%
where the time goes in v1:
time: 890 us; the launch traced here: 880 us
  blocking collectives  321 us (36%)
  waiting for transfers between devices  231 us (26%)
  starting transfers between devices  122 us (14%)
  matrix products  87.1 us (10%)
  other arithmetic  57.1 us (6%)
  local copies, waits for them, and re-layouts  44 us (5%)
  between operations  16.1 us (2%)
    psum x2, blocking collectives, shards(): summed = lax.psum(lax.psum((d_first, d_middle, d_last), 'view'), 'slab')  273 us
    psum x2, waiting for transfers between devices, shards(): summed = lax.psum(lax.psum((d_first, d_middle, d_last), 'view'), 'slab')  200 us
    ppermute x12, starting transfers between devices, with_halo(): lax.ppermute(tail, axis, [(i, (i + 1) % count) for i in range(ends)])  101 us
    all_gather x1, blocking collectives, shards(): piece = lax.all_gather(strip_grad, 'view', axis=1, tiled=True)  48.3 us
    dot_general x81, matrix products, kernel_grad(): jnp.einsum('ozyx,czyx->oc', dout, parts[xc][:, za:za + depth, yb:yb + row...  48 us
    scatter-add x16, other arithmetic, fold_add_view(): jax.ops.segment_sum(jnp.take(proj, source.reshape(-1), axis=0), target.re...  38.8 us
    dot_general x135, matrix products, convolve(): jnp.einsum('oc,czyx->ozyx', kernel[za, yb, xc], parts[xc][:, za:za + dept...  38.6 us
    ppermute x12, waiting for transfers between devices, with_halo(): lax.ppermute(head, axis, [((i + 1) % count, i) for i in range(ends)])  25.2 us
  transfers between devices with their start and end apart: 27, of which 10 were waited for; matrix products, arithmetic and copies ran while one was open for 7% of the time, Pallas kernels for 0%

profile of v1, /device:TPU:1, one launch (start us, length us, event | category | flops | bytes accessed | tf_op | source)
XLA Modules:
  0.0 880.0 jit_solution(795080830807781845)
XLA Ops:
  7.3 3.5 copy.388
  10.8 2.7 copy.389
  15.8 21.8 %while.30 = (s32[]{:T(128)}, f32[4,32,1,128]{3,2,1,0:T(1,128)S(1)}, s32[16,4,32,1,2]{4,2,1,3,0:T(8,128)S(1)}, s32[16,4,32,1,2]{4,2,1,3,0:T(8,128)S(1)}, f32[512,...) while((s32[]{:T(128)}, f32[4,32,1,128]{3,2,1,0:T(1,128)S(1)}, ...), condition=%wide.region_2.3_spmd.clone, body=%wide.region_0.2_spmd.clone.sunk | while | flops 86788 | bytes 669307 | solution.py:104
  38.3 4.4 collective-permute-start
  44.9 2.4 collective-permute-done.1
  47.3 6.5 collective-permute-start.2
  53.8 1.9 collective-permute-start.3
  55.7 4.6 collective-permute-done.3
  68.0 5.2 reduce-scatter.2.cloned.1.call-done
  73.9 3.2 collective-permute-start.4
  78.7 2.8 collective-permute-done.5
  81.6 4.7 collective-permute-start.6
  88.3 4.6 collective-permute-done.7
  106.4 3.2 collective-permute-start.8
  112.4 2.8 collective-permute-done.9
  115.2 3.1 collective-permute-start.10
  120.3 4.9 collective-permute-done.11
  154.0 4.8 collective-permute-start.20
  164.2 4.3 collective-permute-start.12
  170.4 2.4 collective-permute-start.22
  172.9 2.5 collective-permute-start.23
  176.1 4.6 collective-permute-start.14
  180.6 2.1 collective-permute-start.15
  183.6 28.1 %all-reduce.17.cloned.1.call-done = f32[3,3,3,32,32]{4,3,2,1,0:T(8,128)} async-done(((f32[3,3,3,32,32]{4,3,2,1,0:T(8,128)}), f32[3,3,3,32,32]{4,3,2,1,0:T(8,128)}) %all-reduce.17.cloned.1.call-update) | async-done | bytes 110608 | tf_op jit(solution)/shard_map/psum | solution.py:156
  250.6 16.2 %all-reduce.13 = (f32[3,3,3,32,6]{3,4,2,1,0:T(8,128)S(1)}, f32[3,3,3,5,32]{4,2,3,1,0:T(4,128)S(1)}) all-reduce(f32[3,3,3,32,6]{3,4,2,1,0:T(8,128)} %bitcast.559, f32[3,3,3,5,32]{4,2,3,1,0:T(4,128)S(1)} %copy.582), channel_id=1, replica_groups=mesh['slab'=64,'view'=4] {'view'}, use_global_device_ids=true, to_apply=%region_7.8 | all-reduce | flops 9504 | bytes 76032 | tf_op jit(solution)/shard_map/psum | solution.py:156
  266.9 256.4 %all-reduce.12 = (f32[3,3,3,32,6]{3,4,2,1,0:T(8,128)S(1)}, f32[3,3,3,5,32]{4,2,3,1,0:T(4,128)S(1)}) all-reduce(f32[3,3,3,32,6]{3,4,2,1,0:T(8,128)S(1)} %get-tuple-element.301, f32[3,3,3,5,32]{4,2,3,1,0:T(4,128)S(1)} %get-tuple-element.302), channel_id=1, replica_groups=mesh['slab'=64,'view'=4] {'slab'}, use_global_device_ids=true, to_apply=%region_8.9 | all-reduce | flops 9504 | bytes 76032 | tf_op jit(solution)/shard_map/psum | solution.py:156
  527.3 3.0 collective-permute-done.17
  530.3 58.9 %collective-permute-start.18 = (bf16[32,6,1,128]{3,0,2,1:T(8,128)(2,1)S(1)}, bf16[32,6,1,128]{3,0,2,1:T(8,128)(2,1)S(1)}, u32[]{:S(2)}, u32[]{:S(2)}) collective-permute-start(bf16[32,6,1,128]{3,0,2,1:T(8,128)(2,1)S(1)} %get-tuple-element.365), channel_id=1, source_target_pairs={{0,1},{1,2},{2,3},{4,5},{5,6},{6,7},{8,9},{9,10},{10,11},{12,13},{... | collective-permute-start | bytes 147464 | tf_op jit(solution)/shard_map/ppermute | solution.py:16
  589.2 2.1 collective-permute-start.19
  591.4 172.2 %all-reduce.19.cloned.1.call-done = f32[3,3,3,32,32]{4,3,2,1,0:T(8,128)} async-done(((f32[3,3,3,32,32]{4,3,2,1,0:T(8,128)}), f32[3,3,3,32,32]{4,3,2,1,0:T(8,128)}) %all-reduce.19.cloned.1.call-update) | async-done | bytes 110608 | tf_op jit(solution)/shard_map/psum | solution.py:156
  770.8 48.3 %all-gather = bf16[1,4,32,128]{3,0,2,1:T(2,128)(2,1)S(1)} all-gather(bf16[1,4,8,128]{3,0,2,1:T(2,128)(2,1)S(1)} %slice.2106), channel_id=2, replica_groups=mesh['slab'=64,'view'=4] {'view'}, dimensions={2}, use_global_device_ids=true | all-gather | bytes 40960 | tf_op jit(solution)/shard_map/all_gather | solution.py:135
  819.5 53.1 %while.29 = (s32[]{:T(128)}, f32[64,128]{1,0:T(8,128)S(1)}, s32[16,4,32,1,2]{4,2,1,3,0:T(8,128)S(1)}, s32[16,4,32,1,2]{4,2,1,3,0:T(8,128)S(1)}, f32[1024,128]{1,...) while((s32[]{:T(128)}, f32[64,128]{1,0:T(8,128)S(1)}, ...), condition=%wide.region_6.7_spmd.clone.clone, body=%wide.region_4.6_spmd.clone.clone.sunk | while | flops 70019 | bytes 588653 | solution.py:153
  820.4 2.4 scatter_custom_fusion.6
  823.7 2.4 scatter_custom_fusion.6
  827.0 2.4 scatter_custom_fusion.6
  830.3 2.4 scatter_custom_fusion.6
  833.7 2.4 scatter_custom_fusion.6
  837.0 2.4 scatter_custom_fusion.6
  840.3 2.4 scatter_custom_fusion.6
  843.6 2.4 scatter_custom_fusion.6
  846.9 2.4 scatter_custom_fusion.6
  850.2 2.4 scatter_custom_fusion.6
  853.6 2.4 scatter_custom_fusion.6
  856.9 2.4 scatter_custom_fusion.6
  860.2 2.4 scatter_custom_fusion.6
  863.5 2.4 scatter_custom_fusion.6
  866.8 2.4 scatter_custom_fusion.6
  870.1 2.4 scatter_custom_fusion.6
  (735 shorter events, 156.8 us)
Async XLA Ops:
  7.2 66.0 %reduce-scatter.2.cloned.1.call-start = ((), (), s32[]{:S(2)}) async-start(), calls=%async_computation.1 | async-start | bytes 81920 | tf_op jit(solution)/shard_map/reduce_scatter | solution.py:107
  15.7 22.5 %copy-start.6 = (f32[5,4,8,128]{3,2,1,0:T(8,128)S(1)}, f32[5,4,8,128]{3,2,1,0:T(8,128)}, u32[]{:S(2)}) copy-start(f32[5,4,8,128]{3,2,1,0:T(8,128)} %param.21) | copy-start | bytes 245764
  15.7 28.2 %copy-start.60 = (bf16[3,3,3,5,32]{4,2,3,1,0:T(4,128)(2,1)S(1)}, bf16[3,3,3,5,32]{4,2,3,1,0:T(4,128)(2,1)}, u32[]{:S(2)}) copy-start(bf16[3,3,3,5,32]{4,2,3,1,0:T(4,128)(2,1)} %param.20) | copy-start | bytes 25924
  15.8 28.3 %copy-start.5 = (bf16[3,3,3,32,32]{4,3,2,1,0:T(8,128)(2,1)S(1)}, bf16[3,3,3,32,32]{4,3,2,1,0:T(8,128)(2,1)}, u32[]{:S(2)}) copy-start(bf16[3,3,3,32,32]{4,3,2,1,0:T(8,128)(2,1)} %param.19) | copy-start | bytes 165892
  15.8 28.5 %copy-start.51 = (bf16[3,3,3,32,6]{3,4,2,1,0:T(8,128)(2,1)S(1)}, bf16[3,3,3,32,6]{3,4,2,1,0:T(8,128)(2,1)}, u32[]{:S(2)}) copy-start(bf16[3,3,3,32,6]{3,4,2,1,0:T(8,128)(2,1)} %param.18) | copy-start | bytes 31108
  15.8 29.1 %copy-start.55 = (f32[5,4,8,128]{3,2,1,0:T(8,128)S(1)}, f32[5,4,8,128]{3,2,1,0:T(8,128)}, u32[]{:S(2)}) copy-start(f32[5,4,8,128]{3,2,1,0:T(8,128)} %param.13) | copy-start | bytes 245764
  38.2 173.4 %all-reduce.17.cloned.1.call-start = ((), (), s32[]{:S(2)}) async-start(), calls=%async_computation.2 | async-start | bytes 884736 | tf_op jit(solution)/shard_map/psum | solution.py:156
  38.3 6.6 collective-permute-start
  42.7 4.6 collective-permute-start.1
  44.0 34.4 %copy-start.53 = (bf16[3,3,3,32,5]{3,4,2,1,0:T(8,128)(2,1)}, bf16[3,3,3,32,5]{3,4,2,1,0:T(8,128)(2,1)S(1)}, u32[]{:S(2)}) copy-start(bf16[3,3,3,32,5]{3,4,2,1,0:T(8,128)(2,1)S(1)} %reverse_bitcast_fusion.2) | copy-start | bytes 25924
  47.3 8.4 collective-permute-start.2
  53.8 6.6 collective-permute-start.3
  73.9 4.8 collective-permute-start.4
  77.1 4.4 collective-permute-start.5
  78.4 21.2 %copy-start.52 = (bf16[3,3,3,32,6]{3,4,2,1,0:T(8,128)(2,1)S(1)}, bf16[3,3,3,32,6]{3,4,2,1,0:T(8,128)(2,1)}, u32[]{:S(2)}) copy-start(bf16[3,3,3,32,6]{3,4,2,1,0:T(8,128)(2,1)} %param.18) | copy-start | bytes 31108
  81.6 6.7 collective-permute-start.6
  86.3 6.6 collective-permute-start.7
  88.3 12.0 %copy-start.17 = (bf16[6,4,8,128]{3,2,1,0:T(8,128)(2,1)}, bf16[6,4,8,128]{3,2,1,0:T(8,128)(2,1)S(1)}, u32[]{:S(2)}) copy-start(bf16[6,4,8,128]{3,2,1,0:T(8,128)(2,1)S(1)} %get-tuple-element.448) | copy-start | bytes 147460
  106.4 5.9 collective-permute-start.8
  109.6 5.6 collective-permute-start.9
  115.2 5.1 collective-permute-start.10
  118.3 6.9 collective-permute-start.11
  154.0 15.7 %collective-permute-start.20 = (bf16[32,1,8,128]{3,0,2,1:T(8,128)(2,1)}, bf16[32,1,8,128]{3,0,2,1:T(8,128)(2,1)S(1)}, u32[]{:S(2)}, u32[]{:S(2)}) collective-permute-start(bf16[32,1,8,128]{3,0,2,1:T(8,128)(2,1)} %get-tuple-element.377), channel_id=1, source_target_pairs={{0,4},{4,8},{8,12},{12,16},{16,20},{20,24},{24,28},{28,32},{32,36}... | collective-permute-start | bytes 196616 | tf_op jit(solution)/shard_map/ppermute | solution.py:16
  158.9 10.9 %collective-permute-start.21 = (bf16[32,1,8,128]{3,0,2,1:T(8,128)(2,1)}, bf16[32,1,8,128]{3,0,2,1:T(8,128)(2,1)S(1)}, u32[]{:S(2)}, u32[]{:S(2)}) collective-permute-start(bf16[32,1,8,128]{3,0,2,1:T(8,128)(2,1)} %get-tuple-element.378), channel_id=1, source_target_pairs={{4,0},{8,4},{12,8},{16,12},{20,16},{24,20},{28,24},{32,28},{36,32}... | collective-permute-start | bytes 196616 | tf_op jit(solution)/shard_map/ppermute | solution.py:18
  164.1 599.5 %all-reduce.19.cloned.1.call-start = ((), (), s32[]{:S(2)}) async-start(), calls=%async_computation.3 | async-start | bytes 884736 | tf_op jit(solution)/shard_map/psum | solution.py:156
  164.2 11.2 %collective-permute-start.12 = (bf16[32,1,8,128]{3,0,2,1:T(8,128)(2,1)}, bf16[32,1,8,128]{3,0,2,1:T(8,128)(2,1)S(1)}, u32[]{:S(2)}, u32[]{:S(2)}) collective-permute-start(bf16[32,1,8,128]{3,0,2,1:T(8,128)(2,1)} %get-tuple-element.381), channel_id=1, source_target_pairs={{0,4},{4,8},{8,12},{12,16},{16,20},{20,24},{24,28},{28,32},{32,36}... | collective-permute-start | bytes 196616 | tf_op jit(solution)/shard_map/ppermute | solution.py:16
  168.5 6.9 collective-permute-start.13
  170.4 51.3 %collective-permute-start.22 = (bf16[32,6,1,128]{3,0,2,1:T(8,128)(2,1)}, bf16[32,6,1,128]{3,0,2,1:T(8,128)(2,1)}, u32[]{:S(2)}, u32[]{:S(2)}) collective-permute-start(bf16[32,6,1,128]{3,0,2,1:T(8,128)(2,1)} %get-tuple-element.363), channel_id=1, source_target_pairs={{0,1},{1,2},{2,3},{4,5},{5,6},{6,7},{8,9},{9,10},{10,11},{12,13},{... | collective-permute-start | bytes 147464 | tf_op jit(solution)/shard_map/ppermute | solution.py:16
  172.9 48.8 %collective-permute-start.23 = (bf16[32,6,1,128]{3,0,2,1:T(8,128)(2,1)}, bf16[32,6,1,128]{3,0,2,1:T(8,128)(2,1)}, u32[]{:S(2)}, u32[]{:S(2)}) collective-permute-start(bf16[32,6,1,128]{3,0,2,1:T(8,128)(2,1)} %get-tuple-element.364), channel_id=1, source_target_pairs={{1,0},{2,1},{3,2},{5,4},{6,5},{7,6},{9,8},{10,9},{11,10},{13,12},{... | collective-permute-start | bytes 147464 | tf_op jit(solution)/shard_map/ppermute | solution.py:18
  176.1 35.6 %collective-permute-start.14 = (bf16[32,6,1,128]{3,0,2,1:T(8,128)(2,1)}, bf16[32,6,1,128]{3,0,2,1:T(8,128)(2,1)}, u32[]{:S(2)}, u32[]{:S(2)}) collective-permute-start(bf16[32,6,1,128]{3,0,2,1:T(8,128)(2,1)} %get-tuple-element.369), channel_id=1, source_target_pairs={{0,1},{1,2},{2,3},{4,5},{5,6},{6,7},{8,9},{9,10},{10,11},{12,13},{... | collective-permute-start | bytes 147464 | tf_op jit(solution)/shard_map/ppermute | solution.py:16
  180.6 31.0 %collective-permute-start.15 = (bf16[32,6,1,128]{3,0,2,1:T(8,128)(2,1)}, bf16[32,6,1,128]{3,0,2,1:T(8,128)(2,1)}, u32[]{:S(2)}, u32[]{:S(2)}) collective-permute-start(bf16[32,6,1,128]{3,0,2,1:T(8,128)(2,1)} %get-tuple-element.370), channel_id=1, source_target_pairs={{1,0},{2,1},{3,2},{5,4},{6,5},{7,6},{9,8},{10,9},{11,10},{13,12},{... | collective-permute-start | bytes 147464 | tf_op jit(solution)/shard_map/ppermute | solution.py:18
  228.9 11.6 %copy-start.28 = (bf16[6,4,8,128]{3,2,1,0:T(8,128)(2,1)S(1)}, bf16[6,4,8,128]{3,2,1,0:T(8,128)(2,1)}, u32[]{:S(2)}) copy-start(bf16[6,4,8,128]{3,2,1,0:T(8,128)(2,1)} %copy-done.27) | copy-start | bytes 147460
  229.1 12.2 %copy-start.8 = (bf16[6,4,8,128]{3,2,1,0:T(8,128)(2,1)S(1)}, bf16[6,4,8,128]{3,2,1,0:T(8,128)(2,1)}, u32[]{:S(2)}) copy-start(bf16[6,4,8,128]{3,2,1,0:T(8,128)(2,1)} %copy-done.7) | copy-start | bytes 147460
  229.3 12.8 %copy-start.34 = (bf16[6,4,8,128]{3,2,1,0:T(8,128)(2,1)S(1)}, bf16[6,4,8,128]{3,2,1,0:T(8,128)(2,1)}, u32[]{:S(2)}) copy-start(bf16[6,4,8,128]{3,2,1,0:T(8,128)(2,1)} %copy-done.33) | copy-start | bytes 147460
  229.5 13.3 %copy-start.24 = (bf16[6,4,8,128]{3,2,1,0:T(8,128)(2,1)S(1)}, bf16[6,4,8,128]{3,2,1,0:T(8,128)(2,1)}, u32[]{:S(2)}) copy-start(bf16[6,4,8,128]{3,2,1,0:T(8,128)(2,1)} %copy-done.23) | copy-start | bytes 147460
  229.8 14.5 %copy-start.12 = (bf16[6,4,8,128]{3,2,1,0:T(8,128)(2,1)S(1)}, bf16[6,4,8,128]{3,2,1,0:T(8,128)(2,1)}, u32[]{:S(2)}) copy-start(bf16[6,4,8,128]{3,2,1,0:T(8,128)(2,1)} %copy-done.11) | copy-start | bytes 147460
  230.0 15.1 %copy-start.20 = (bf16[6,4,8,128]{3,2,1,0:T(8,128)(2,1)S(1)}, bf16[6,4,8,128]{3,2,1,0:T(8,128)(2,1)}, u32[]{:S(2)}) copy-start(bf16[6,4,8,128]{3,2,1,0:T(8,128)(2,1)} %copy-done.19) | copy-start | bytes 147460
  231.1 16.4 %copy-start.10 = (bf16[6,4,8,128]{3,2,1,0:T(8,128)(2,1)S(1)}, bf16[6,4,8,128]{3,2,1,0:T(8,128)(2,1)}, u32[]{:S(2)}) copy-start(bf16[6,4,8,128]{3,2,1,0:T(8,128)(2,1)} %copy-done.9) | copy-start | bytes 147460
  232.6 16.4 %copy-start.14 = (bf16[6,4,8,128]{3,2,1,0:T(8,128)(2,1)S(1)}, bf16[6,4,8,128]{3,2,1,0:T(8,128)(2,1)}, u32[]{:S(2)}) copy-start(bf16[6,4,8,128]{3,2,1,0:T(8,128)(2,1)} %copy-done.13) | copy-start | bytes 147460
  233.4 16.4 %copy-start.59 = (bf16[6,4,8,128]{3,2,1,0:T(8,128)(2,1)S(1)}, bf16[6,4,8,128]{3,2,1,0:T(8,128)(2,1)}, u32[]{:S(2)}) copy-start(bf16[6,4,8,128]{3,2,1,0:T(8,128)(2,1)} %copy-done.58) | copy-start | bytes 147460
  235.8 289.4 %copy-start.57 = (bf16[32,1,8,128]{3,0,2,1:T(8,128)(2,1)S(1)}, bf16[32,1,8,128]{3,0,2,1:T(8,128)(2,1)}, u32[]{:S(2)}) copy-start(bf16[32,1,8,128]{3,0,2,1:T(8,128)(2,1)} %get-tuple-element.380) | copy-start | bytes 196612
  235.8 290.7 %copy-start.54 = (bf16[3,3,3,6,32]{4,3,2,1,0:T(8,128)(2,1)S(1)}, bf16[3,3,3,6,32]{4,3,2,1,0:T(8,128)(2,1)}, u32[]{:S(2)}) copy-start(bf16[3,3,3,6,32]{4,3,2,1,0:T(8,128)(2,1)} %reverse_bitcast_fusion.1) | copy-start | bytes 31108
  523.9 3.4 collective-permute-start.16
  525.2 5.1 collective-permute-start.17
  530.3 235.1 %collective-permute-start.18 = (bf16[32,6,1,128]{3,0,2,1:T(8,128)(2,1)S(1)}, bf16[32,6,1,128]{3,0,2,1:T(8,128)(2,1)S(1)}, u32[]{:S(2)}, u32[]{:S(2)}) collective-permute-start(bf16[32,6,1,128]{3,0,2,1:T(8,128)(2,1)S(1)} %get-tuple-element.365), channel_id=1, source_target_pairs={{0,1},{1,2},{2,3},{4,5},{5,6},{6,7},{8,9},{9,10},{10,11},{12,13},{... | collective-permute-start | bytes 147464 | tf_op jit(solution)/shard_map/ppermute | solution.py:16
  589.2 176.2 %collective-permute-start.19 = (bf16[32,6,1,128]{3,0,2,1:T(8,128)(2,1)S(1)}, bf16[32,6,1,128]{3,0,2,1:T(8,128)(2,1)S(1)}, u32[]{:S(2)}, u32[]{:S(2)}) collective-permute-start(bf16[32,6,1,128]{3,0,2,1:T(8,128)(2,1)S(1)} %get-tuple-element.366), channel_id=1, source_target_pairs={{1,0},{2,1},{3,2},{5,4},{6,5},{7,6},{9,8},{10,9},{11,10},{13,12},{... | collective-permute-start | bytes 147464 | tf_op jit(solution)/shard_map/ppermute | solution.py:18
  769.1 50.0 %copy-start.4 = (bf16[8,128,128]{2,1,0:T(8,128)(2,1)S(1)}, bf16[8,128,128]{2,1,0:T(8,128)(2,1)}, u32[]{:S(2)}) copy-start(bf16[8,128,128]{2,1,0:T(8,128)(2,1)} %param.15) | copy-start | bytes 786436
  819.2 54.1 %copy-start.1 = (bf16[16,4,128]{2,1,0:T(4,128)(2,1)S(1)}, bf16[16,4,128]{2,1,0:T(4,128)(2,1)}, u32[]{:S(2)}) copy-start(bf16[16,4,128]{2,1,0:T(4,128)(2,1)} %param.14) | copy-start | bytes 49156
  (43 other events, 259.4 us)
Sparse Core Ops, SparseCore 0:
  38.3 34.8 reduce-scatter.1
  164.3 47.3 all-reduce.16
  214.3 549.3 all-reduce.18
